TPU v7x, 32 devices: a whole 2x2x4 slice. The times are simulated.
32 devices in a mesh: blk: 8 (over z, y), chan: 4 (over x, core).
Axes of the slice: x: 2, y: 2, z: 4, core: 2. Of those that a mesh axis runs over, the one named last changes fastest.
Arguments:
- hidden_in: bfloat16 [2, 1, 2048, 768], P(None, None, ('blk', 'chan')), may hold values from -6 to 6
- cotangent: bfloat16 [2, 1, 2048, 768], P(None, None, ('blk', 'chan')), may hold values from -6 to 6
- mixer_input_weight: bfloat16 [768, 2304], P(None, ('blk', 'chan')), may hold values from -0.21875 to 0.21875
- mixer_output_weight: bfloat16 [768, 768], P(None, ('blk', 'chan')), may hold values from -0.21875 to 0.21875
- feedforward_up: bfloat16 [768, 3072], P(None, ('blk', 'chan')), may hold values from -0.21875 to 0.21875
- feedforward_down: bfloat16 [3072, 768], P(('blk', 'chan')), may hold values from -0.109375 to 0.109375
- first_gain: bfloat16 [768], P(('blk', 'chan')), may hold values from 0.5 to 1.5
- first_shift: bfloat16 [768], P(('blk', 'chan')), may hold values from -3 to 3
- second_gain: bfloat16 [768], P(('blk', 'chan')), may hold values from 0.5 to 1.5
- second_shift: bfloat16 [768], P(('blk', 'chan')), may hold values from -3 to 3
- short_taps: bfloat16 [3, 3, 768], P(None, None, ('blk', 'chan')), may hold values from -4 to 4
- short_bias: bfloat16 [3, 768], P(None, ('blk', 'chan')), may hold values from -3 to 3
- skip_scale: bfloat16 [768], P(('blk', 'chan')), may hold values from -4 to 4
- filter_out: bfloat16 [64, 768], P(None, ('blk', 'chan')), may hold values from -0.023925781 to 0.023925781
- pos_weight: bfloat16 [33, 64], replicated, may hold values from -1 to 1
- pos_bias: bfloat16 [64], replicated, may hold values from -4 to 4
- mid_weight: bfloat16 [64, 64], replicated, may hold values from -0.75 to 0.75
- mid_bias: bfloat16 [64], replicated, may hold values from -4 to 4
- sine_freq: bfloat16 [64], replicated, may hold values from 2 to 16
- decay_rate: bfloat16 [768], P(('blk', 'chan')), may hold values from 0.00024414062 to 0.029907227
Outputs:
- hidden_out: bfloat16 [2, 1, 2048, 768], P(None, None, ('blk', 'chan'))
- grad_hidden: bfloat16 [2, 1, 2048, 768], P(None, None, ('blk', 'chan'))
- grad_mixer_in: float32 [768, 2304], P(None, ('blk', 'chan'))
- grad_mixer_out: float32 [768, 768], P(None, ('blk', 'chan'))
- grad_mlp_up: float32 [768, 3072], P(None, ('blk', 'chan'))
- grad_mlp_down: float32 [3072, 768], P(('blk', 'chan'))
- grad_first_gain: float32 [768], P(('blk', 'chan'))
- grad_first_shift: float32 [768], P(('blk', 'chan'))
- grad_second_gain: float32 [768], P(('blk', 'chan'))
- grad_second_shift: float32 [768], P(('blk', 'chan'))
- grad_short_taps: float32 [3, 3, 768], P(None, None, ('blk', 'chan'))
- grad_short_bias: float32 [3, 768], P(None, ('blk', 'chan'))
- grad_skip_scale: float32 [768], P(('blk', 'chan'))
- grad_filter_out: float32 [64, 768], P(None, ('blk', 'chan'))
- grad_pos_weight: float32 [33, 64], replicated
- grad_pos_bias: float32 [64], replicated
- grad_mid_weight: float32 [64, 64], replicated
- grad_mid_bias: float32 [64], replicated
- grad_sine_freq: float32 [64], replicated
All inputs are finite; a program needn't handle non-finite values.
Results may differ from a plain program's by a relative error of at most 0.012.
Values may be sent and summed in bfloat16 or wider, within the bound.
A program may use at most 320 MiB of HBM per device.

v0:
```python
import math
import jax
import jax.numpy as jnp
from jax import lax
from jax.sharding import PartitionSpec as P

EPS = 1e-05
BANDS = 16
EXACT = lax.Precision.HIGHEST
AXES = ("blk", "chan")
F32 = jnp.float32
BF16 = jnp.bfloat16


def contract(a, b, dim_a, dim_b, precision=None):
    return lax.dot_general(
        a, b, (((dim_a,), (dim_b,)), ((), ())), precision=precision, preferred_element_type=F32
    )


def positions(length):
    lags = jnp.arange(length).astype(F32)
    band_freq = 0.0001 + (BANDS - 1 - 0.0001) * jnp.arange(BANDS).astype(F32) / (BANDS - 1)
    phase = 2.0 * math.pi / length * lags[None, :] * band_freq[:, None]
    return (
        lags,
        jnp.concatenate([lags[None, :] / (length - 1), jnp.cos(phase), -jnp.sin(phase)], 0),
    )


def filter_hidden(length, pos_weight, pos_bias, mid_weight, mid_bias, sine_freq):
    lags, features = positions(length)
    freq = sine_freq[:, None]
    first_sum = contract(pos_weight, features, 0, 0, EXACT) + pos_bias[:, None]
    first = jnp.sin(freq * first_sum)
    second_sum = contract(mid_weight, first, 0, 0, EXACT) + mid_bias[:, None]
    second = jnp.sin(freq * second_sum)
    return (lags, features, first_sum, first, second_sum, second)


def block_table(block):
    spot = lax.broadcasted_iota(jnp.int32, (block, block), 0)
    freq = lax.broadcasted_iota(jnp.int32, (block, block), 1)
    phase = math.pi / block * (spot * freq % (2 * block)).astype(F32)
    parity = 1.0 - 2.0 * (spot % 2).astype(F32)
    imag = jnp.where(freq == 0, parity, -jnp.sin(phase))
    return jnp.concatenate([jnp.cos(phase), imag], 1)


def to_spectrum(blocks, table):
    spec = lax.dot_general(
        blocks,
        table,
        (((blocks.ndim - 1,), (0,)), ((), ())),
        precision=EXACT,
        preferred_element_type=F32,
    )
    half = table.shape[0]
    return (spec[..., :half], spec[..., half:])


def from_spectrum(real, imag, table):
    half = table.shape[0]
    weight = jnp.where(lax.iota(jnp.int32, half) == 0, 0.5 / half, 1.0 / half)
    spec = jnp.concatenate([real * weight, imag * weight], -1)
    return lax.dot_general(
        spec,
        table,
        (((spec.ndim - 1,), (1,)), ((), ())),
        precision=EXACT,
        preferred_element_type=F32,
    )


def packed_kernel(real, imag):
    first = lax.iota(jnp.int32, real.shape[-1]) == 0
    return (real, jnp.where(first, imag, real), jnp.where(first, 0.0, imag))


def layer_norm(values, gain, shift):
    center = values - jnp.mean(values, -1, keepdims=True)
    scale_inv = lax.rsqrt(jnp.mean(center * center, -1, keepdims=True) + EPS)
    normal = center * scale_inv
    return (normal * gain + shift, normal, scale_inv)


def layer_norm_back(grad_out, normal, scale_inv, gain):
    grad_normal = grad_out * gain
    inner = grad_normal - jnp.mean(grad_normal, -1, keepdims=True)
    inner = inner - normal * jnp.mean(grad_normal * normal, -1, keepdims=True)
    return (inner * scale_inv, jnp.sum(grad_out * normal, 0), jnp.sum(grad_out, 0))


def gelu_parts(v):
    root = math.sqrt(2.0 / math.pi)
    inner = root * (v + 0.044715 * v * v * v)
    t = jnp.tanh(inner)
    value = 0.5 * v * (1.0 + t)
    slope = 0.5 * (1.0 + t) + 0.5 * v * (1.0 - t * t) * root * (1.0 + 3.0 * 0.044715 * v * v)
    return (value, slope)


def delayed(values, steps):
    if steps == 0:
        return values
    pad = jnp.zeros(values.shape[:-1] + (steps,), values.dtype)
    return jnp.concatenate([pad, values[..., :-steps]], -1)


def advanced(values, steps):
    if steps == 0:
        return values
    pad = jnp.zeros(values.shape[:-1] + (steps,), values.dtype)
    return jnp.concatenate([values[..., steps:], pad], -1)


def exchange(values):
    return lax.all_to_all(values, AXES, split_axis=0, concat_axis=0, tiled=True)


def shards(
    hidden_in,
    cotangent,
    mixer_input_weight,
    mixer_output_weight,
    feedforward_up,
    feedforward_down,
    first_gain,
    first_shift,
    second_gain,
    second_shift,
    short_taps,
    short_bias,
    skip_scale,
    filter_out,
    pos_weight,
    pos_bias,
    mid_weight,
    mid_bias,
    sine_freq,
    decay_rate,
):
    devices = lax.axis_size(AXES)
    micro, seq_count, tok, width = hidden_in.shape
    seqs = micro * seq_count
    tokens = seqs * tok
    length = tok * devices
    chans = width // devices
    block = tok * lax.axis_size("chan")
    blocks = length // block

    def gather(shard):
        return lax.all_gather(shard, AXES, axis=0, tiled=True)

    rows_in, rows_out, rows_up = (
        w.shape[1] for w in (mixer_input_weight, mixer_output_weight, feedforward_up)
    )
    weight_in = gather(mixer_input_weight.T)
    weight_out = gather(mixer_output_weight.T)
    weight_up = gather(feedforward_up.T)
    weight_down = gather(feedforward_down)
    norms = jnp.stack([first_gain, first_shift, second_gain, second_shift])
    norms = lax.all_gather(norms, AXES, axis=1, tiled=True).astype(F32)
    gain_one, shift_one, gain_two, shift_two = (norms[0], norms[1], norms[2], norms[3])
    freq = sine_freq.astype(F32)
    w_pos, w_mid, w_fil = (pos_weight.astype(F32), mid_weight.astype(F32), filter_out.astype(F32))
    lags, features, first_sum, first_act, second_sum, second_act = filter_hidden(
        length, w_pos, pos_bias.astype(F32), w_mid, mid_bias.astype(F32), freq
    )
    decay = jnp.exp(-lags[None, :] * decay_rate.astype(F32)[:, None])
    kernel = contract(w_fil, second_act, 0, 0, EXACT) * decay
    table = block_table(block)
    sign = 1.0 - 2.0 * (lax.iota(jnp.int32, block) % 2).astype(F32)
    ker_re, ker_im = to_spectrum(kernel.reshape(chans, blocks, block), table)

    def with_previous(spec):
        before = jnp.concatenate([jnp.zeros_like(spec[:, :1]), spec[:, :-1]], 1)
        return spec + sign * before

    k_re, k_alt, k_im = packed_kernel(with_previous(ker_re), with_previous(ker_im))
    values = hidden_in.reshape(tokens, width).astype(F32)
    normed, normal_one, inv_one = layer_norm(values, gain_one, shift_one)
    normed = normed.astype(BF16)
    projected = contract(weight_in, normed, 1, 1).astype(BF16)
    projected = projected.reshape(3, devices, chans, tokens).transpose(1, 0, 2, 3)
    arrived = exchange(projected)

    def by_sequence(values):
        parts = values.shape[1]
        values = values.reshape(devices, parts, chans, seqs, tok)
        return values.transpose(1, 3, 2, 0, 4).reshape(parts, seqs, chans, length)

    def by_device(values):
        parts = values.shape[0]
        values = values.reshape(parts, seqs, chans, devices, tok)
        return values.transpose(3, 0, 2, 1, 4).reshape(devices, parts, chans, tokens)

    steps = by_sequence(arrived).astype(F32)
    taps = short_taps.astype(F32)[:, :, None, :, None]
    conv = short_bias.astype(F32)[:, None, :, None]
    for i in range(3):
        conv = conv + taps[i] * delayed(steps, i)
    gate_out, gate_in, signal = (conv[0], conv[1], conv[2])
    gated = signal * gate_in
    sig_re, sig_im = to_spectrum(gated.reshape(seqs, chans, blocks, block), table)

    def shifted_sum(make):
        total = None
        for d in range(blocks):
            term = make(d)
            total = term if total is None else tuple((a + b for a, b in zip(total, term)))
        return total

    def ahead(x, d):
        return x if d == 0 else jnp.pad(x[:, :, :-d], ((0, 0), (0, 0), (d, 0), (0, 0)))

    def back(x, d):
        return x if d == 0 else jnp.pad(x[:, :, d:], ((0, 0), (0, 0), (0, d), (0, 0)))

    def forward_term(d):
        re, im = (ahead(sig_re, d), ahead(sig_im, d))
        kr, ka, ki = (k_re[:, d : d + 1], k_alt[:, d : d + 1], k_im[:, d : d + 1])
        return (re * kr - im * ki, re * ki + im * ka)

    out_re, out_im = shifted_sum(forward_term)
    long_out = from_spectrum(out_re, out_im, table).reshape(seqs, chans, length)
    skip = skip_scale.astype(F32)[None, :, None]
    long_total = long_out + skip * gated
    mixed = (long_total * gate_out).astype(BF16)
    mixed = exchange(by_device(mixed[None])).reshape(width, tokens)
    resid = values + contract(mixed, weight_out, 0, 1)
    second, normal_two, inv_two = layer_norm(resid, gain_two, shift_two)
    second = second.astype(BF16)
    upper = contract(second, weight_up, 1, 1)
    active, slope = gelu_parts(upper)
    active = active.astype(BF16)
    result = resid + contract(active, weight_down, 1, 0)
    cot = cotangent.reshape(tokens, width)
    grad_down = contract(active, cot, 0, 0)
    grad_upper = (contract(cot, weight_down, 1, 1) * slope).astype(BF16)
    grad_up = contract(grad_upper, second, 0, 0)
    grad_second = contract(grad_upper, weight_up, 1, 0)
    resid_term, grad_gain_two, grad_shift_two = layer_norm_back(
        grad_second, normal_two, inv_two, gain_two
    )
    grad_resid = cot.astype(F32) + resid_term
    grad_branch = grad_resid.astype(BF16)
    grad_out_w = contract(grad_branch, mixed, 0, 1)
    grad_mixed = contract(weight_out, grad_branch, 0, 1).astype(BF16)
    grad_mixed = exchange(grad_mixed.reshape(devices, 1, chans, tokens))
    grad_mixed = by_sequence(grad_mixed)[0].astype(F32)
    grad_gate_out = grad_mixed * long_total
    grad_long = grad_mixed * gate_out
    grad_skip = jnp.sum(grad_long * gated, (0, 2))
    gl_re, gl_im = to_spectrum(grad_long.reshape(seqs, chans, blocks, block), table)

    def signal_term(d):
        re, im = (back(gl_re, d), back(gl_im, d))
        kr, ka, ki = (k_re[:, d : d + 1], k_alt[:, d : d + 1], k_im[:, d : d + 1])
        return (re * kr + im * ki, im * ka - re * ki)

    gg_re, gg_im = shifted_sum(signal_term)
    grad_gated = from_spectrum(gg_re, gg_im, table).reshape(seqs, chans, length) + skip * grad_long
    first_slot = lax.iota(jnp.int32, block) == 0
    kg_re, kg_im = ([], [])
    for d in range(blocks):
        s_re, s_im = (sig_re[:, :, : blocks - d], sig_im[:, :, : blocks - d])
        g_re, g_im = (gl_re[:, :, d:], gl_im[:, :, d:])
        same, other = (g_re * s_re, g_im * s_im)
        kg_re.append(jnp.sum(jnp.where(first_slot, same, same + other), (0, 2)))
        kg_im.append(jnp.sum(jnp.where(first_slot, other, g_im * s_re - g_re * s_im), (0, 2)))
    kg_re, kg_im = (jnp.stack(kg_re, 1), jnp.stack(kg_im, 1))

    def with_next(spec):
        after = jnp.concatenate([spec[:, 1:], jnp.zeros_like(spec[:, :1])], 1)
        return spec + sign * after

    grad_kernel = from_spectrum(with_next(kg_re), with_next(kg_im), table).reshape(chans, length)
    grad_conv = jnp.stack([grad_gate_out, grad_gated * signal, grad_gated * gate_in])
    grad_bias = jnp.sum(grad_conv, (1, 3))
    grad_taps = jnp.stack([jnp.sum(grad_conv * delayed(steps, i), (1, 3)) for i in range(3)])
    grad_steps = taps[0] * grad_conv
    for i in (1, 2):
        grad_steps = grad_steps + taps[i] * advanced(grad_conv, i)
    grad_proj = exchange(by_device(grad_steps.astype(BF16)))
    grad_proj = grad_proj.transpose(1, 0, 2, 3).reshape(3 * width, tokens)
    fade = grad_kernel * decay
    grad_filter = contract(second_act, fade, 1, 1, EXACT)
    grad_two = contract(w_fil, fade, 1, 0, EXACT) * jnp.cos(freq[:, None] * second_sum)
    grad_freq = jnp.sum(grad_two * second_sum, 1)
    grad_two = grad_two * freq[:, None]
    grad_mid = contract(first_act, grad_two, 1, 1, EXACT)
    grad_one = contract(w_mid, grad_two, 1, 0, EXACT) * jnp.cos(freq[:, None] * first_sum)
    grad_freq = grad_freq + jnp.sum(grad_one * first_sum, 1)
    grad_one = grad_one * freq[:, None]
    grad_pos = contract(features, grad_one, 1, 1, EXACT)
    small = lax.psum(
        jnp.concatenate(
            [
                grad_pos,
                jnp.sum(grad_one, 1)[None],
                grad_mid,
                jnp.sum(grad_two, 1)[None],
                grad_freq[None],
            ]
        ),
        AXES,
    )
    emb, order = pos_weight.shape
    grad_in = contract(grad_proj, normed, 1, 0)
    grad_normed = contract(grad_proj, weight_in, 0, 0)
    input_term, grad_gain_one, grad_shift_one = layer_norm_back(
        grad_normed, normal_one, inv_one, gain_one
    )
    grad_hidden = (grad_resid + input_term).astype(BF16)

    def reduce_rows(partial):
        return lax.psum_scatter(partial.astype(BF16), AXES, scatter_dimension=0, tiled=True).astype(
            F32
        )

    norm_grads = jnp.stack([grad_gain_one, grad_shift_one, grad_gain_two, grad_shift_two])
    norm_grads = lax.psum_scatter(norm_grads, AXES, scatter_dimension=1, tiled=True)
    return (
        result.astype(BF16).reshape(hidden_in.shape),
        grad_hidden.reshape(hidden_in.shape),
        reduce_rows(grad_in).T,
        reduce_rows(grad_out_w).T,
        reduce_rows(grad_up).T,
        reduce_rows(grad_down),
        norm_grads[0],
        norm_grads[1],
        norm_grads[2],
        norm_grads[3],
        grad_taps,
        grad_bias,
        grad_skip,
        grad_filter,
        small[:emb],
        small[emb],
        small[emb + 1 : emb + 1 + order],
        small[emb + 1 + order],
        small[emb + 2 + order],
    )


def solution(mesh):
    rows, spread, tokens = (P(AXES), P(None, AXES), P(None, None, AXES, None))
    params = (
        rows,
        rows,
        rows,
        rows,
        P(None, None, AXES),
        spread,
        rows,
        spread,
        P(),
        P(),
        P(),
        P(),
        P(),
    )
    return jax.shard_map(
        shards,
        mesh=mesh,
        in_specs=(tokens, tokens, spread, spread, spread, P(AXES, None)) + params + (rows,),
        out_specs=(tokens, tokens, spread, spread, spread, P(AXES, None)) + params,
        check_vma=False,
    )
```

profile of v0, /device:TPU:0, one launch (start us, length us, event | category | flops | bytes accessed | tf_op | source)
XLA Modules:
  0.0 719.1 jit_solution(14635279991504066053)
XLA Ops:
  13.0 43.4 %all-gather = bf16[32,24,4]{1,2,0:T(4,128)(2,1)S(1)} all-gather(bf16[1,24,4]{1,2,0:T(4,128)(2,1)S(1)} %maximum_bitcast_fusion), channel_id=1, replica_groups=mesh['blk'=8,'chan'=4] {'blk','chan'}, dimensions={0}, use_global_device_ids=true | all-gather | bytes 6336 | tf_op jit(solution)/shard_map/all_gather | solution.py:163
  73.7 3.3 fusion.1
  78.2 3.7 all-to-all-start
  123.5 3.8 all-to-all-start.1
  127.3 3.1 all-gather.8.cloned.1.call-done
  130.4 5.8 all-to-all-done.1
  138.4 57.5 %all-gather.10.cloned.1.call-done = bf16[3072,768]{1,0:T(8,128)(2,1)} async-done(((bf16[96,768]{1,0:T(8,128)(2,1)}), bf16[3072,768]{1,0:T(8,128)(2,1)}) %all-gather.10.cloned.1.call-update) | async-done | bytes 4718608 | tf_op jit(solution)/shard_map/all_gather | solution.py:153
  195.9 5.3 fusion.123
  201.2 60.0 %all-gather.12.cloned.1.call-done = bf16[3072,768]{1,0:T(8,128)(2,1)} async-done(((bf16[96,768]{1,0:T(8,128)(2,1)}), bf16[3072,768]{1,0:T(8,128)(2,1)}) %all-gather.12.cloned.1.call-update) | async-done | bytes 4718608 | tf_op jit(solution)/shard_map/all_gather | solution.py:153
  261.1 4.8 fusion
  271.4 3.5 all-to-all-start.2
  280.2 3.6 all-to-all-done.2
  318.0 3.3 reshape.376
  325.0 18.6 %all-to-all-done.3 = bf16[32,3,24,128]{3,2,1,0:T(8,128)(2,1)S(1)} async-done(((bf16[32,3,24,128]{3,2,1,0:T(8,128)(2,1)}), bf16[32,3,24,128]{3,2,1,0:T(8,128)(2,1)S(1)}, u32[]{:S(2)}, u32[]{:S(2)}) %all-to-all-start.3) | async-done | bytes 589856 | tf_op jit(solution)/shard_map/all_to_all | solution.py:118
  343.6 4.0 convolution_convert_fusion.2
  348.8 3.7 convolution_convert_fusion.1
  353.4 5.3 convolution_convert_fusion
  359.4 4.6 fusion.13
  375.0 3.5 multiply_reduce_fusion.3
  386.7 3.8 fusion.2
  396.8 39.7 %all-reduce.37 = (f32[4,768]{1,0:T(4,128)S(1)}, f32[100,64]{0,1:T(8,128)S(1)}) all-reduce(f32[4,768]{1,0:T(4,128)S(1)} %pad_maximum_fusion.11, f32[100,64]{0,1:T(8,128)S(1)} %concatenate.60), channel_id=6, replica_groups=mesh['blk'=8,'chan'=4] {'blk','chan'}, use_global_device_ids=true, to_apply=%region_16.17.clone | all-reduce | flops 9472 | bytes 75776
  441.6 44.7 %reduce-scatter.6.cloned.1.call-done = bf16[72,768]{1,0:T(8,128)(2,1)} async-done(((bf16[2304,768]{1,0:T(8,128)(2,1)}), bf16[72,768]{1,0:T(8,128)(2,1)}) %reduce-scatter.6.cloned.1.call-update) | async-done | bytes 110608 | tf_op jit(solution)/shard_map/reduce_scatter | solution.py:318
  487.9 109.8 %reduce-scatter.10.cloned.1.call-done = bf16[96,768]{1,0:T(8,128)(2,1)} async-done(((bf16[3072,768]{1,0:T(8,128)(2,1)}), bf16[96,768]{1,0:T(8,128)(2,1)}) %reduce-scatter.10.cloned.1.call-update) | async-done | bytes 147472 | tf_op jit(solution)/shard_map/reduce_scatter | solution.py:318
  599.3 110.9 %reduce-scatter.12.cloned.1.call-done = bf16[96,768]{1,0:T(8,128)(2,1)} async-done(((bf16[3072,768]{1,0:T(8,128)(2,1)}), bf16[96,768]{1,0:T(8,128)(2,1)}) %reduce-scatter.12.cloned.1.call-update) | async-done | bytes 147472 | tf_op jit(solution)/shard_map/reduce_scatter | solution.py:318
  (509 shorter events, 152.7 us)
Async XLA Ops:
  7.2 55.4 %copy-start = (bf16[64,64]{1,0:T(8,128)(2,1)S(1)}, bf16[64,64]{1,0:T(8,128)(2,1)}, u32[]{:S(2)}) copy-start(bf16[64,64]{1,0:T(8,128)(2,1)} %param.36) | copy-start | bytes 24580
  7.2 66.5 %all-gather.6.cloned.1.call-start = ((), (), s32[]{:S(2)}) async-start(), calls=%async_computation.8 | async-start | bytes 3649536 | tf_op jit(solution)/shard_map/all_gather | solution.py:153
  7.9 122.4 %all-gather.8.cloned.1.call-start = ((), (), s32[]{:S(2)}) async-start(), calls=%async_computation.9 | async-start | bytes 1216512 | tf_op jit(solution)/shard_map/all_gather | solution.py:153
  8.7 187.2 %all-gather.10.cloned.1.call-start = ((), (), s32[]{:S(2)}) async-start(), calls=%async_computation.10 | async-start | bytes 4866048 | tf_op jit(solution)/shard_map/all_gather | solution.py:153
  8.7 56.0 %copy-start.119 = (bf16[64,24]{0,1:T(8,128)(2,1)S(1)}, bf16[64,24]{0,1:T(8,128)(2,1)}, u32[]{:S(2)}) copy-start(bf16[64,24]{0,1:T(8,128)(2,1)} %param.33) | copy-start | bytes 9220
  9.4 251.7 %all-gather.12.cloned.1.call-start = ((), (), s32[]{:S(2)}) async-start(), calls=%async_computation.11 | async-start | bytes 4866048 | tf_op jit(solution)/shard_map/all_gather | solution.py:153
  12.3 57.9 %copy-start.139 = (f32[128]{0:T(128)}, f32[128]{0:T(128)S(1)}, u32[]{:S(2)}) copy-start(f32[128]{0:T(128)S(1)} %div.40) | copy-start | bytes 1540
  12.3 54.6 %copy-start.106 = (f32[1,2048]{1,0:T(1,128)}, f32[1,2048]{1,0:T(1,128)S(1)}, u32[]{:S(2)}) copy-start(f32[1,2048]{1,0:T(1,128)S(1)} %convert_multiply_fusion.1) | copy-start | bytes 24580
  67.0 15.0 %copy-start.108 = (pred[256]{0:T(512)(128)(4,1)}, pred[256]{0:T(512)(128)(4,1)S(1)}, u32[]{:S(2)}) copy-start(pred[256]{0:T(512)(128)(4,1)S(1)} %get-tuple-element.236) | copy-start | bytes 772
  67.6 14.4 %copy-start.133 = (f32[256]{0:T(256)}, f32[256]{0:T(256)S(1)}, u32[]{:S(2)}) copy-start(f32[256]{0:T(256)S(1)} %get-tuple-element.239) | copy-start | bytes 3076
  70.2 46.5 %copy-start.8 = (f32[256,256]{1,0:T(8,128)}, f32[256,256]{1,0:T(8,128)S(1)}, u32[]{:S(2)}) copy-start(f32[256,256]{1,0:T(8,128)S(1)} %negate_select_fusion.2) | copy-start | bytes 786436
  78.2 21.3 %all-to-all-start = ((bf16[32,3,24,128]{3,2,1,0:T(8,128)(2,1)}), bf16[32,3,24,128]{3,2,1,0:T(8,128)(2,1)}, u32[]{:S(2)}, u32[]{:S(2)}) async-start(bf16[32,3,24,128]{3,2,1,0:T(8,128)(2,1)} %copy.120), calls=%async_computation | async-start | bytes 1179648 | tf_op jit(solution)/shard_map/all_to_all | solution.py:118
  123.5 12.7 %all-to-all-start.1 = ((bf16[32,1,24,128]{3,2,1,0:T(8,128)(2,1)}), bf16[32,1,24,128]{3,2,1,0:T(8,128)(2,1)S(1)}, u32[]{:S(2)}, u32[]{:S(2)}) async-start(bf16[32,1,24,128]{3,2,1,0:T(8,128)(2,1)} %bitcast.23), calls=%async_computation.1 | async-start | bytes 393216 | tf_op jit(solution)/shard_map/all_to_all | solution.py:118
  136.2 65.0 %copy-start.39 = (bf16[32,1,24,128]{3,2,1,0:T(8,128)(2,1)}, bf16[32,1,24,128]{3,2,1,0:T(8,128)(2,1)S(1)}, u32[]{:S(2)}) copy-start(bf16[32,1,24,128]{3,2,1,0:T(8,128)(2,1)S(1)} %all-to-all-done.1) | copy-start | bytes 589828
  138.2 129.3 %copy-start.129 = (f32[128]{0:T(128)}, f32[128]{0:T(128)S(1)}, u32[]{:S(2)}) copy-start(f32[128]{0:T(128)S(1)} %broadcast_multiply_fusion.5) | copy-start | bytes 1540
  138.4 129.1 %copy-start.135 = (f32[128]{0:T(128)}, f32[128]{0:T(128)S(1)}, u32[]{:S(2)}) copy-start(f32[128]{0:T(128)S(1)} %add_rsqrt_fusion.1) | copy-start | bytes 1540
  195.9 65.2 %copy-start.45 = (bf16[2,1,64,768]{3,2,1,0:T(8,128)(2,1)S(1)}, bf16[2,1,64,768]{3,2,1,0:T(8,128)(2,1)}, u32[]{:S(2)}) copy-start(bf16[2,1,64,768]{3,2,1,0:T(8,128)(2,1)} %param.21) | copy-start | bytes 589828
  271.4 12.4 %all-to-all-start.2 = ((bf16[32,1,24,128]{3,2,1,0:T(8,128)(2,1)}), bf16[32,1,24,128]{3,2,1,0:T(8,128)(2,1)}, u32[]{:S(2)}, u32[]{:S(2)}) async-start(bf16[32,1,24,128]{3,2,1,0:T(8,128)(2,1)} %bitcast.300), calls=%async_computation.2 | async-start | bytes 393216 | tf_op jit(solution)/shard_map/all_to_all | solution.py:118
  275.0 165.2 %reduce-scatter.8.cloned.1.call-start = ((), (), s32[]{:S(2)}) async-start(), calls=%async_computation.13 | async-start | bytes 1216512 | tf_op jit(solution)/shard_map/reduce_scatter | solution.py:318
  321.3 22.2 %all-to-all-start.3 = ((bf16[32,3,24,128]{3,2,1,0:T(8,128)(2,1)}), bf16[32,3,24,128]{3,2,1,0:T(8,128)(2,1)S(1)}, u32[]{:S(2)}, u32[]{:S(2)}) async-start(bf16[32,3,24,128]{3,2,1,0:T(8,128)(2,1)} %reshape.376), calls=%async_computation.3 | async-start | bytes 1179648 | tf_op jit(solution)/shard_map/all_to_all | solution.py:118
  324.0 162.2 %reduce-scatter.6.cloned.1.call-start = ((), (), s32[]{:S(2)}) async-start(), calls=%async_computation.12 | async-start | bytes 3649536 | tf_op jit(solution)/shard_map/reduce_scatter | solution.py:318
  347.7 250.0 %reduce-scatter.10.cloned.1.call-start = ((), (), s32[]{:S(2)}) async-start(), calls=%async_computation.14 | async-start | bytes 4866048 | tf_op jit(solution)/shard_map/reduce_scatter | solution.py:318
  352.5 357.6 %reduce-scatter.12.cloned.1.call-start = ((), (), s32[]{:S(2)}) async-start(), calls=%async_computation.15 | async-start | bytes 4866048 | tf_op jit(solution)/shard_map/reduce_scatter | solution.py:318
  395.9 43.4 %copy-start.23 = (f32[128,768]{1,0:T(8,128)S(1)}, f32[128,768]{1,0:T(8,128)}, u32[]{:S(2)}) copy-start(f32[128,768]{1,0:T(8,128)} %copy-done.22) | copy-start | bytes 1179652
  (138 other events, 393.9 us)
Sparse Core Ops, SparseCore 0:
  10.9 62.7 all-gather.5
  76.6 53.7 all-gather.7
  133.3 62.5 all-gather.9
  198.7 62.4 all-gather.11
  280.6 98.2 reduce-scatter.7
  384.1 102.0 reduce-scatter.5
  491.7 105.8 reduce-scatter.9
  604.0 106.0 reduce-scatter.11
where the time goes:
time: 728 us; the launch traced here: 719 us
  waiting for transfers between devices  422 us (58%)
  blocking collectives  83.1 us (11%)
  local copies, waits for them, and re-layouts  74.8 us (10%)
  matrix products  63.1 us (9%)
  other arithmetic  44.8 us (6%)
  between operations  16.8 us (2%)
  starting transfers between devices  14.3 us (2%)
    reduce_scatter x4, waiting for transfers between devices, reduce_rows(): lax.psum_scatter(partial.astype(BF16), AXES, scatter_dimension=0, tiled=T...  265 us
    all_gather x4, waiting for transfers between devices, gather(): return lax.all_gather(shard, AXES, axis=0, tiled=True)  123 us
    dot_general x20, matrix products, contract(): lax.dot_general(a, b, (((dim_a,), (dim_b,)), ((), ())), precision=precisi...  55.4 us
    all_gather x1, blocking collectives, shards(): norms = lax.all_gather(norms, AXES, axis=1, tiled=True).astype(F32)  43.4 us
    unnamed x1, blocking collectives  39.7 us
    all_to_all x4, waiting for transfers between devices, exchange(): return lax.all_to_all(values, AXES, split_axis=0, concat_axis=0, tiled=True)  31 us
    unnamed x331, local copies, waits for them, and re-layouts  23.3 us
  transfers between devices with their start and end apart: 12, of which 11 were waited for; matrix products, arithmetic and copies ran while one was open for 23% of the time, Pallas kernels for 0%

commit v1 on v0

--- a/solution.py
+++ b/solution.py
@@ -10,6 +10,27 @@
 AXES = ("blk", "chan")
 F32 = jnp.float32
 BF16 = jnp.bfloat16
+
+
+def joined_along(pieces, dim):
+    pieces = jnp.moveaxis(pieces, 0, dim)
+    lengths = pieces.shape
+    return pieces.reshape(*lengths[:dim], lengths[dim] * lengths[dim + 1], *lengths[dim + 2 :])
+
+
+def grow_blocks(array, axis):
+    peers, index = (lax.axis_size(axis), lax.axis_index(axis))
+    parts, stride = (array[None], 1)
+    while stride < peers:
+        theirs = lax.ppermute(parts, axis, [(i, i ^ stride) for i in range(peers)])
+        low = index & stride == 0
+        parts = jnp.concatenate([jnp.where(low, parts, theirs), jnp.where(low, theirs, parts)])
+        stride *= 2
+    return parts
+
+
+def doubled_up(array, axis, dim):
+    return joined_along(grow_blocks(array, axis), dim)
 
 
 def contract(a, b, dim_a, dim_b, precision=None):
@@ -150,7 +171,7 @@
     blocks = length // block
 
     def gather(shard):
-        return lax.all_gather(shard, AXES, axis=0, tiled=True)
+        return doubled_up(shard, AXES, 0)
 
     rows_in, rows_out, rows_up = (
         w.shape[1] for w in (mixer_input_weight, mixer_output_weight, feedforward_up)

time: 728 us -> 916 us (1.26)
  waiting for transfers between devices: 422 us -> 554 us
  other arithmetic: 44.8 us -> 66.9 us
  blocking collectives: 83.1 us -> 105 us
  starting transfers between devices: 14.3 us -> 26.9 us
    ppermute x0 -> x20, waiting for transfers between devices: none -> 188 us  [grow_blocks(): theirs = lax.ppermute(parts, axis, [(i, i ^ stride) for i in range(peers)])]
    all_gather x4 -> x0, waiting for transfers between devices: 123 us -> none  [gather(): return lax.all_gather(shard, AXES, axis=0, tiled=True)]
    all_to_all x4 -> x3, waiting for transfers between devices: 31 us -> 99.2 us  [exchange(): return lax.all_to_all(values, AXES, split_axis=0, concat_axis=0, tiled=True)]
    all_to_all x0 -> x1, blocking collectives: none -> 21.9 us  [exchange(): return lax.all_to_all(values, AXES, split_axis=0, concat_axis=0, tiled=True)]
    ppermute x0 -> x20, starting transfers between devices: none -> 14 us  [grow_blocks(): theirs = lax.ppermute(parts, axis, [(i, i ^ stride) for i in range(peers)])]
    concatenate x0 -> x20, other arithmetic: none -> 14 us  [grow_blocks(): jnp.concatenate([jnp.where(low, parts, theirs), jnp.where(low, theirs, pa...]
    select_n x0 -> x19, other arithmetic: none -> 9.21 us  [grow_blocks(): jnp.where(low, parts, theirs)]
    unnamed x331 -> x377, local copies, waits for them, and re-layouts: 23.3 us -> 26.4 us
  transfers between devices with their start and end apart: 12 -> 27, of which waited for: 11 -> 16; matrix products, arithmetic and copies ran while one was open for 23% -> 20% of each run, Pallas kernels for 0% -> 0%
where the time goes in v1:
time: 916 us; the launch traced here: 905 us
  waiting for transfers between devices  554 us (60%)
  blocking collectives  105 us (11%)
  local copies, waits for them, and re-layouts  78.9 us (9%)
  other arithmetic  66.9 us (7%)
  matrix products  56.1 us (6%)
  starting transfers between devices  26.9 us (3%)
  between operations  17.1 us (2%)
    reduce_scatter x4, waiting for transfers between devices, reduce_rows(): lax.psum_scatter(partial.astype(BF16), AXES, scatter_dimension=0, tiled=T...  267 us
    ppermute x20, waiting for transfers between devices, grow_blocks(): theirs = lax.ppermute(parts, axis, [(i, i ^ stride) for i in range(peers)])  188 us
    all_to_all x3, waiting for transfers between devices, exchange(): return lax.all_to_all(values, AXES, split_axis=0, concat_axis=0, tiled=True)  99.2 us
    dot_general x20, matrix products, contract(): lax.dot_general(a, b, (((dim_a,), (dim_b,)), ((), ())), precision=precisi...  48.5 us
    all_gather x1, blocking collectives, shards(): norms = lax.all_gather(norms, AXES, axis=1, tiled=True).astype(F32)  43.2 us
    unnamed x1, blocking collectives  39.5 us
    unnamed x377, local copies, waits for them, and re-layouts  26.4 us
    all_to_all x1, blocking collectives, exchange(): return lax.all_to_all(values, AXES, split_axis=0, concat_axis=0, tiled=True)  21.9 us
  transfers between devices with their start and end apart: 27, of which 16 were waited for; matrix products, arithmetic and copies ran while one was open for 20% of the time, Pallas kernels for 0%

profile of v1, /device:TPU:0, one launch (start us, length us, event | category | flops | bytes accessed | tf_op | source)
XLA Modules:
  0.0 904.6 jit_solution(3252164599136780005)
XLA Ops:
  10.7 43.2 %all-gather = bf16[32,24,4]{1,2,0:T(4,128)(2,1)S(1)} all-gather(bf16[1,24,4]{1,2,0:T(4,128)(2,1)S(1)} %maximum_bitcast_fusion), channel_id=1, replica_groups=mesh['blk'=8,'chan'=4] {'blk','chan'}, dimensions={0}, use_global_device_ids=true | all-gather | bytes 6336 | tf_op jit(solution)/shard_map/all_gather | solution.py:184
  72.2 6.1 collective-permute-done.1
  101.3 15.5 %collective-permute-done.3 = bf16[8,72,768]{2,1,0:T(8,128)(2,1)S(1)} collective-permute-done((bf16[8,72,768]{2,1,0:T(8,128)(2,1)S(1)}, bf16[8,72,768]{2,1,0:T(8,128)(2,1)S(1)}, u32[]{:S(2)}, u32[]{:S(2)}) %collective-permute-start.3) | collective-permute-done | bytes 884768 | tf_op jit(solution)/shard_map/ppermute | solution.py:25
  124.6 9.1 %collective-permute-done.17 = bf16[4,96,768]{2,1,0:T(8,128)(2,1)S(1)} collective-permute-done((bf16[4,96,768]{2,1,0:T(8,128)(2,1)S(1)}, bf16[4,96,768]{2,1,0:T(8,128)(2,1)S(1)}, u32[]{:S(2)}, u32[]{:S(2)}) %collective-permute-start.17) | collective-permute-done | bytes 589856 | tf_op jit(solution)/shard_map/ppermute | solution.py:25
  134.9 5.9 collective-permute-done.12
  142.6 63.7 %collective-permute-done.4 = bf16[16,72,768]{2,1,0:T(8,128)(2,1)S(1)} collective-permute-done((bf16[16,72,768]{2,1,0:T(8,128)(2,1)S(1)}, bf16[16,72,768]{2,1,0:T(8,128)(2,1)S(1)}, u32[]{:S(2)}, u32[]{:S(2)}) %collective-permute-start.4) | collective-permute-done | bytes 1769504 | tf_op jit(solution)/shard_map/ppermute | solution.py:25
  209.7 4.9 all-to-all-start
  223.6 9.6 %collective-permute-done.13 = bf16[8,96,768]{2,1,0:T(8,128)(2,1)} collective-permute-done((bf16[8,96,768]{2,1,0:T(8,128)(2,1)}, bf16[8,96,768]{2,1,0:T(8,128)(2,1)}, u32[]{:S(2)}, u32[]{:S(2)}) %collective-permute-start.13) | collective-permute-done | bytes 1179680 | tf_op jit(solution)/shard_map/ppermute | solution.py:25
  236.7 95.8 %all-to-all-done = bf16[32,3,24,128]{3,2,1,0:T(8,128)(2,1)} async-done(((bf16[32,3,24,128]{3,2,1,0:T(8,128)(2,1)}), bf16[32,3,24,128]{3,2,1,0:T(8,128)(2,1)}, u32[]{:S(2)}, u32[]{:S(2)}) %all-to-all-start) | async-done | bytes 589856 | tf_op jit(solution)/shard_map/all_to_all | solution.py:139
  358.1 3.7 all-to-all-start.1
  361.9 23.4 %collective-permute-done.19 = bf16[16,96,768]{2,1,0:T(8,128)(2,1)} collective-permute-done((bf16[16,96,768]{2,1,0:T(8,128)(2,1)}, bf16[16,96,768]{2,1,0:T(8,128)(2,1)}, u32[]{:S(2)}, u32[]{:S(2)}) %collective-permute-start.19) | collective-permute-done | bytes 2359328 | tf_op jit(solution)/shard_map/ppermute | solution.py:25
  387.6 48.2 %collective-permute-done.14 = bf16[16,96,768]{2,1,0:T(8,128)(2,1)} collective-permute-done((bf16[16,96,768]{2,1,0:T(8,128)(2,1)}, bf16[16,96,768]{2,1,0:T(8,128)(2,1)}, u32[]{:S(2)}, u32[]{:S(2)}) %collective-permute-start.14) | collective-permute-done | bytes 2359328 | tf_op jit(solution)/shard_map/ppermute | solution.py:25
  445.4 4.1 fusion.122
  456.3 3.7 all-to-all-start.2
  505.7 21.9 %all_to_all.20 = bf16[32,3,24,128]{3,2,1,0:T(8,128)(2,1)S(1)} all-to-all(bf16[32,3,24,128]{3,2,1,0:T(8,128)(2,1)S(1)} %reshape.417), channel_id=1, replica_groups=mesh['blk'=8,'chan'=4] {'blk','chan'}, dimensions={0} | all-to-all | bytes 1179648 | tf_op jit(solution)/shard_map/all_to_all | solution.py:139
  531.7 3.7 convolution_convert_fusion.1
  536.4 5.2 convolution_convert_fusion
  543.9 4.6 fusion.13
  559.4 3.5 multiply_reduce_fusion.3
  571.0 3.8 fusion.2
  581.1 39.5 %all-reduce.37 = (f32[4,768]{1,0:T(4,128)S(1)}, f32[100,64]{0,1:T(8,128)S(1)}) all-reduce(f32[4,768]{1,0:T(4,128)S(1)} %pad_maximum_fusion.31, f32[100,64]{0,1:T(8,128)S(1)} %concatenate.140), channel_id=6, replica_groups=mesh['blk'=8,'chan'=4] {'blk','chan'}, use_global_device_ids=true, to_apply=%region_16.17.clone | all-reduce | flops 9472 | bytes 75776
  625.7 46.4 %reduce-scatter.6.cloned.1.call-done = bf16[72,768]{1,0:T(8,128)(2,1)} async-done(((bf16[2304,768]{1,0:T(8,128)(2,1)}), bf16[72,768]{1,0:T(8,128)(2,1)}) %reduce-scatter.6.cloned.1.call-update) | async-done | bytes 110608 | tf_op jit(solution)/shard_map/reduce_scatter | solution.py:339
  673.7 109.9 %reduce-scatter.10.cloned.1.call-done = bf16[96,768]{1,0:T(8,128)(2,1)} async-done(((bf16[3072,768]{1,0:T(8,128)(2,1)}), bf16[96,768]{1,0:T(8,128)(2,1)}) %reduce-scatter.10.cloned.1.call-update) | async-done | bytes 147472 | tf_op jit(solution)/shard_map/reduce_scatter | solution.py:339
  785.3 110.7 %reduce-scatter.12.cloned.1.call-done = bf16[96,768]{1,0:T(8,128)(2,1)} async-done(((bf16[3072,768]{1,0:T(8,128)(2,1)}), bf16[96,768]{1,0:T(8,128)(2,1)}) %reduce-scatter.12.cloned.1.call-update) | async-done | bytes 147472 | tf_op jit(solution)/shard_map/reduce_scatter | solution.py:339
  (619 shorter events, 201.2 us)
Async XLA Ops:
  7.2 62.7 %collective-permute-start = (bf16[1,72,768]{2,1,0:T(8,128)(2,1)}, bf16[1,72,768]{2,1,0:T(8,128)(2,1)S(1)}, u32[]{:S(2)}, u32[]{:S(2)}) collective-permute-start(bf16[1,72,768]{2,1,0:T(8,128)(2,1)} %bitcast.404), channel_id=1, source_target_pairs={{0,1},{1,0},{2,3},{3,2},{4,5},{5,4},{6,7},{7,6},{8,9},{9,8},{10,11... | collective-permute-start | bytes 331784 | tf_op jit(solution)/shard_map/ppermute | solution.py:25
  7.7 62.4 %collective-permute-start.5 = (bf16[1,24,768]{2,1,0:T(8,128)(2,1)}, bf16[1,24,768]{2,1,0:T(8,128)(2,1)S(1)}, u32[]{:S(2)}, u32[]{:S(2)}) collective-permute-start(bf16[1,24,768]{2,1,0:T(8,128)(2,1)} %bitcast.406), channel_id=1, source_target_pairs={{0,1},{1,0},{2,3},{3,2},{4,5},{5,4},{6,7},{7,6},{8,9},{9,8},{10,11... | collective-permute-start | bytes 110600 | tf_op jit(solution)/shard_map/ppermute | solution.py:25
  7.8 88.3 %collective-permute-start.15 = (bf16[1,96,768]{2,1,0:T(8,128)(2,1)}, bf16[1,96,768]{2,1,0:T(8,128)(2,1)S(1)}, u32[]{:S(2)}, u32[]{:S(2)}) collective-permute-start(bf16[1,96,768]{2,1,0:T(8,128)(2,1)} %bitcast.402), channel_id=1, source_target_pairs={{0,1},{1,0},{2,3},{3,2},{4,5},{5,4},{6,7},{7,6},{8,9},{9,8},{10,11... | collective-permute-start | bytes 442376 | tf_op jit(solution)/shard_map/ppermute | solution.py:25
  8.2 87.8 %collective-permute-start.10 = (bf16[1,96,768]{2,1,0:T(8,128)(2,1)}, bf16[1,96,768]{2,1,0:T(8,128)(2,1)S(1)}, u32[]{:S(2)}, u32[]{:S(2)}) collective-permute-start(bf16[1,96,768]{2,1,0:T(8,128)(2,1)} %bitcast.403), channel_id=1, source_target_pairs={{0,1},{1,0},{2,3},{3,2},{4,5},{5,4},{6,7},{7,6},{8,9},{9,8},{10,11... | collective-permute-start | bytes 442376 | tf_op jit(solution)/shard_map/ppermute | solution.py:25
  70.2 23.5 %collective-permute-start.6 = (bf16[2,24,768]{2,1,0:T(8,128)(2,1)S(1)}, bf16[2,24,768]{2,1,0:T(8,128)(2,1)S(1)}, u32[]{:S(2)}, u32[]{:S(2)}) collective-permute-start(bf16[2,24,768]{2,1,0:T(8,128)(2,1)S(1)} %pad_maximum_fusion.24), channel_id=1, source_target_pairs={{0,2},{1,3},{2,0},{3,1},{4,6},{5,7},{6,4},{7,5},{8,10},{9,11},{10,... | collective-permute-start | bytes 221192 | tf_op jit(solution)/shard_map/ppermute | solution.py:25
  78.4 15.3 %collective-permute-start.2 = (bf16[4,72,768]{2,1,0:T(8,128)(2,1)S(1)}, bf16[4,72,768]{2,1,0:T(8,128)(2,1)S(1)}, u32[]{:S(2)}, u32[]{:S(2)}) collective-permute-start(bf16[4,72,768]{2,1,0:T(8,128)(2,1)S(1)} %pad_maximum_fusion.15), channel_id=1, source_target_pairs={{0,4},{1,5},{2,6},{3,7},{4,0},{5,1},{6,2},{7,3},{8,12},{9,13},{10,... | collective-permute-start | bytes 1327112 | tf_op jit(solution)/shard_map/ppermute | solution.py:25
  93.9 23.0 %collective-permute-start.3 = (bf16[8,72,768]{2,1,0:T(8,128)(2,1)S(1)}, bf16[8,72,768]{2,1,0:T(8,128)(2,1)S(1)}, u32[]{:S(2)}, u32[]{:S(2)}) collective-permute-start(bf16[8,72,768]{2,1,0:T(8,128)(2,1)S(1)} %pad_maximum_fusion.10), channel_id=1, source_target_pairs={{0,8},{1,9},{2,10},{3,11},{4,12},{5,13},{6,14},{7,15},{8,0},{9,1},... | collective-permute-start | bytes 2654216 | tf_op jit(solution)/shard_map/ppermute | solution.py:25
  96.2 21.1 %collective-permute-start.16 = (bf16[2,96,768]{2,1,0:T(8,128)(2,1)S(1)}, bf16[2,96,768]{2,1,0:T(8,128)(2,1)S(1)}, u32[]{:S(2)}, u32[]{:S(2)}) collective-permute-start(bf16[2,96,768]{2,1,0:T(8,128)(2,1)S(1)} %pad_maximum_fusion.19), channel_id=1, source_target_pairs={{0,2},{1,3},{2,0},{3,1},{4,6},{5,7},{6,4},{7,5},{8,10},{9,11},{10,... | collective-permute-start | bytes 884744 | tf_op jit(solution)/shard_map/ppermute | solution.py:25
  96.3 23.0 %collective-permute-start.11 = (bf16[2,96,768]{2,1,0:T(8,128)(2,1)S(1)}, bf16[2,96,768]{2,1,0:T(8,128)(2,1)S(1)}, u32[]{:S(2)}, u32[]{:S(2)}) collective-permute-start(bf16[2,96,768]{2,1,0:T(8,128)(2,1)S(1)} %pad_maximum_fusion.18), channel_id=1, source_target_pairs={{0,2},{1,3},{2,0},{3,1},{4,6},{5,7},{6,4},{7,5},{8,10},{9,11},{10,... | collective-permute-start | bytes 884744 | tf_op jit(solution)/shard_map/ppermute | solution.py:25
  99.3 22.9 %collective-permute-start.8 = (bf16[8,24,768]{2,1,0:T(8,128)(2,1)S(1)}, bf16[8,24,768]{2,1,0:T(8,128)(2,1)S(1)}, u32[]{:S(2)}, u32[]{:S(2)}) collective-permute-start(bf16[8,24,768]{2,1,0:T(8,128)(2,1)S(1)} %pad_maximum_fusion.17), channel_id=1, source_target_pairs={{0,8},{1,9},{2,10},{3,11},{4,12},{5,13},{6,14},{7,15},{8,0},{9,1},... | collective-permute-start | bytes 884744 | tf_op jit(solution)/shard_map/ppermute | solution.py:25
  117.2 89.1 %collective-permute-start.4 = (bf16[16,72,768]{2,1,0:T(8,128)(2,1)S(1)}, bf16[16,72,768]{2,1,0:T(8,128)(2,1)S(1)}, u32[]{:S(2)}, u32[]{:S(2)}) collective-permute-start(bf16[16,72,768]{2,1,0:T(8,128)(2,1)S(1)} %pad_maximum_fusion.5), channel_id=1, source_target_pairs={{0,16},{1,17},{2,18},{3,19},{4,20},{5,21},{6,22},{7,23},{8,24},{9,... | collective-permute-start | bytes 5308424 | tf_op jit(solution)/shard_map/ppermute | solution.py:25
  117.4 16.3 %collective-permute-start.17 = (bf16[4,96,768]{2,1,0:T(8,128)(2,1)S(1)}, bf16[4,96,768]{2,1,0:T(8,128)(2,1)S(1)}, u32[]{:S(2)}, u32[]{:S(2)}) collective-permute-start(bf16[4,96,768]{2,1,0:T(8,128)(2,1)S(1)} %pad_maximum_fusion.13), channel_id=1, source_target_pairs={{0,4},{1,5},{2,6},{3,7},{4,0},{5,1},{6,2},{7,3},{8,12},{9,13},{10,... | collective-permute-start | bytes 1769480 | tf_op jit(solution)/shard_map/ppermute | solution.py:25
  119.4 21.4 %collective-permute-start.12 = (bf16[4,96,768]{2,1,0:T(8,128)(2,1)S(1)}, bf16[4,96,768]{2,1,0:T(8,128)(2,1)S(1)}, u32[]{:S(2)}, u32[]{:S(2)}) collective-permute-start(bf16[4,96,768]{2,1,0:T(8,128)(2,1)S(1)} %pad_maximum_fusion.12), channel_id=1, source_target_pairs={{0,4},{1,5},{2,6},{3,7},{4,0},{5,1},{6,2},{7,3},{8,12},{9,13},{10,... | collective-permute-start | bytes 1769480 | tf_op jit(solution)/shard_map/ppermute | solution.py:25
  123.1 94.5 %collective-permute-start.9 = (bf16[16,24,768]{2,1,0:T(8,128)(2,1)}, bf16[16,24,768]{2,1,0:T(8,128)(2,1)}, u32[]{:S(2)}, u32[]{:S(2)}) collective-permute-start(bf16[16,24,768]{2,1,0:T(8,128)(2,1)} %pad_maximum_fusion.11), channel_id=1, source_target_pairs={{0,16},{1,17},{2,18},{3,19},{4,20},{5,21},{6,22},{7,23},{8,24},{9,... | collective-permute-start | bytes 1769480 | tf_op jit(solution)/shard_map/ppermute | solution.py:25
  134.9 85.0 %collective-permute-start.18 = (bf16[8,96,768]{2,1,0:T(8,128)(2,1)}, bf16[8,96,768]{2,1,0:T(8,128)(2,1)}, u32[]{:S(2)}, u32[]{:S(2)}) collective-permute-start(bf16[8,96,768]{2,1,0:T(8,128)(2,1)} %pad_maximum_fusion.8), channel_id=1, source_target_pairs={{0,8},{1,9},{2,10},{3,11},{4,12},{5,13},{6,14},{7,15},{8,0},{9,1},... | collective-permute-start | bytes 3538952 | tf_op jit(solution)/shard_map/ppermute | solution.py:25
  142.1 91.1 %collective-permute-start.13 = (bf16[8,96,768]{2,1,0:T(8,128)(2,1)}, bf16[8,96,768]{2,1,0:T(8,128)(2,1)}, u32[]{:S(2)}, u32[]{:S(2)}) collective-permute-start(bf16[8,96,768]{2,1,0:T(8,128)(2,1)} %pad_maximum_fusion.7), channel_id=1, source_target_pairs={{0,8},{1,9},{2,10},{3,11},{4,12},{5,13},{6,14},{7,15},{8,0},{9,1},... | collective-permute-start | bytes 3538952 | tf_op jit(solution)/shard_map/ppermute | solution.py:25
  209.7 122.9 %all-to-all-start = ((bf16[32,3,24,128]{3,2,1,0:T(8,128)(2,1)}), bf16[32,3,24,128]{3,2,1,0:T(8,128)(2,1)}, u32[]{:S(2)}, u32[]{:S(2)}) async-start(bf16[32,3,24,128]{3,2,1,0:T(8,128)(2,1)} %bitcast.321), calls=%async_computation | async-start | bytes 1179648 | tf_op jit(solution)/shard_map/all_to_all | solution.py:139
  223.6 161.7 %collective-permute-start.19 = (bf16[16,96,768]{2,1,0:T(8,128)(2,1)}, bf16[16,96,768]{2,1,0:T(8,128)(2,1)}, u32[]{:S(2)}, u32[]{:S(2)}) collective-permute-start(bf16[16,96,768]{2,1,0:T(8,128)(2,1)} %pad_maximum_fusion.4), channel_id=1, source_target_pairs={{0,16},{1,17},{2,18},{3,19},{4,20},{5,21},{6,22},{7,23},{8,24},{9,... | collective-permute-start | bytes 7077896 | tf_op jit(solution)/shard_map/ppermute | solution.py:25
  236.7 199.1 %collective-permute-start.14 = (bf16[16,96,768]{2,1,0:T(8,128)(2,1)}, bf16[16,96,768]{2,1,0:T(8,128)(2,1)}, u32[]{:S(2)}, u32[]{:S(2)}) collective-permute-start(bf16[16,96,768]{2,1,0:T(8,128)(2,1)} %pad_maximum_fusion.3), channel_id=1, source_target_pairs={{0,16},{1,17},{2,18},{3,19},{4,20},{5,21},{6,22},{7,23},{8,24},{9,... | collective-permute-start | bytes 7077896 | tf_op jit(solution)/shard_map/ppermute | solution.py:25
  358.1 84.9 %all-to-all-start.1 = ((bf16[32,1,24,128]{3,2,1,0:T(8,128)(2,1)}), bf16[32,1,24,128]{3,2,1,0:T(8,128)(2,1)}, u32[]{:S(2)}, u32[]{:S(2)}) async-start(bf16[32,1,24,128]{3,2,1,0:T(8,128)(2,1)} %bitcast.331), calls=%async_computation.1 | async-start | bytes 393216 | tf_op jit(solution)/shard_map/all_to_all | solution.py:139
  460.0 164.4 %reduce-scatter.8.cloned.1.call-start = ((), (), s32[]{:S(2)}) async-start(), calls=%async_computation.9 | async-start | bytes 1216512 | tf_op jit(solution)/shard_map/reduce_scatter | solution.py:339
  465.2 206.9 %reduce-scatter.6.cloned.1.call-start = ((), (), s32[]{:S(2)}) async-start(), calls=%async_computation.8 | async-start | bytes 3649536 | tf_op jit(solution)/shard_map/reduce_scatter | solution.py:339
  530.6 253.1 %reduce-scatter.10.cloned.1.call-start = ((), (), s32[]{:S(2)}) async-start(), calls=%async_computation.10 | async-start | bytes 4866048 | tf_op jit(solution)/shard_map/reduce_scatter | solution.py:339
  535.5 360.5 %reduce-scatter.12.cloned.1.call-start = ((), (), s32[]{:S(2)}) async-start(), calls=%async_computation.11 | async-start | bytes 4866048 | tf_op jit(solution)/shard_map/reduce_scatter | solution.py:339
  (176 other events, 1256.2 us)
Sparse Core Ops, SparseCore 0:
  465.9 98.4 reduce-scatter.7
  569.8 102.2 reduce-scatter.5
  677.6 105.9 reduce-scatter.9
  789.9 106.0 reduce-scatter.11
